TPU v7x, 32 devices: a whole 2x2x4 slice. The times are simulated.
32 devices in a mesh: expert: 8 (over z, x), tensor: 4 (over y, core).
Axes of the slice: x: 2, y: 2, z: 4, core: 2. Of those that a mesh axis runs over, the one named last changes fastest.
Arguments:
- tokens: bfloat16 [8192, 2048], P(('expert', 'tensor')), may hold values from -6 to 6
- cotangent: bfloat16 [8192, 2048], P(('expert', 'tensor')), may hold values from -6 to 6
- routes: int32 [8192, 8], P(('expert', 'tensor')), may hold values from 0 to 15, all different within a row; in each aligned block of 256 rows (0 to 255, 256 to 511, ...) at most 170 rows name the same one
- norm_in: float32 [2048], replicated, may hold values from 0.5 to 1.5
- query_w: bfloat16 [2048, 2048], P(None, 'tensor'), may hold values from -0.125 to 0.125
- key_w: bfloat16 [2048, 2048], P(None, 'tensor'), may hold values from -0.125 to 0.125
- value_w: bfloat16 [2048, 2048], P(None, 'tensor'), may hold values from -0.125 to 0.125
- out_w: bfloat16 [2048, 2048], P('tensor'), may hold values from -1 to 1
- query_gain: float32 [128], replicated, may hold values from 0.1 to 1.9
- key_gain: float32 [128], replicated, may hold values from 0.1 to 1.9
- norm_mid: float32 [2048], replicated, may hold values from 0.5 to 1.5
- router_w: float32 [2048, 16], replicated, may hold values from -0.0625 to 0.0625
- gate_w: bfloat16 [16, 2048, 1024], P('expert'), may hold values from -0.125 to 0.125
- up_w: bfloat16 [16, 2048, 1024], P('expert'), may hold values from -0.125 to 0.125
- down_w: bfloat16 [16, 1024, 2048], P('expert'), may hold values from -0.875 to 0.875
Outputs:
- output: bfloat16 [8192, 2048], P(('expert', 'tensor'))
- input_grad: float32 [8192, 2048], P(('expert', 'tensor'))
- norm_in_grad: float32 [2048], replicated
- query_w_grad: float32 [2048, 2048], P('expert', 'tensor')
- key_w_grad: float32 [2048, 2048], P('expert', 'tensor')
- value_w_grad: float32 [2048, 2048], P('expert', 'tensor')
- out_w_grad: float32 [2048, 2048], P('tensor', 'expert')
- query_gain_grad: float32 [128], replicated
- key_gain_grad: float32 [128], replicated
- norm_mid_grad: float32 [2048], replicated
- router_w_grad: float32 [2048, 16], replicated
- gate_w_grad: float32 [16, 2048, 1024], P('expert', None, 'tensor')
- up_w_grad: float32 [16, 2048, 1024], P('expert', None, 'tensor')
- down_w_grad: float32 [16, 1024, 2048], P('expert', 'tensor')
Inputs may be any that keep to these rules, and one draw needn't show every extreme that they name: `routes`: each row names 8 different experts. Among the 256 rows of one device (aligned blocks), no expert is named by more than 170 rows, and in some block one expert is named by exactly 170.
All inputs are finite; a program needn't handle non-finite values.
Results may differ from a plain program's by a relative error of at most 0.02.
Values may be sent and summed in bfloat16 or wider, within the bound.
A program may use at most 320 MiB of HBM per device.

v0:
```python
import math
import jax
import jax.numpy as jnp
from jax import lax
from jax.sharding import PartitionSpec as P

epsilon = 1e-06
highest = lax.Precision.HIGHEST
contract_last = (((1,), (1,)), ((), ()))
contract_first = (((0,), (0,)), ((), ()))


def inverse_rms(values):
    return lax.rsqrt(jnp.mean(values * values, axis=-1, keepdims=True) + epsilon)


def norm_backward(grad_norm, values, inverse, norm_gain):
    weighted = grad_norm * norm_gain
    inner_mean = jnp.mean(weighted * values, axis=-1, keepdims=True)
    return inverse * weighted - values * inverse * inverse * inverse * inner_mean


def rotary_tables(length, head_width):
    half_dim = head_width // 2
    frequency = jnp.exp(
        -math.log(10000.0) * 2.0 * jnp.arange(half_dim, dtype=jnp.float32) / head_width
    )
    angles = jnp.arange(length, dtype=jnp.float32)[:, None] * frequency[None, :]
    return (jnp.cos(angles)[:, None, :], jnp.sin(angles)[:, None, :])


def rotate(values, cosine, sine_table):
    half_dim = values.shape[-1] // 2
    first_half = values[..., :half_dim]
    second_half = values[..., half_dim:]
    return jnp.concatenate(
        [
            first_half * cosine - second_half * sine_table,
            second_half * cosine + first_half * sine_table,
        ],
        axis=-1,
    )


def rotate_back(gradient, cosine, sine_table):
    half_dim = gradient.shape[-1] // 2
    first_half = gradient[..., :half_dim]
    second_half = gradient[..., half_dim:]
    return jnp.concatenate(
        [
            first_half * cosine + second_half * sine_table,
            second_half * cosine - first_half * sine_table,
        ],
        axis=-1,
    )


def swiglu_back(hidden_grad, gate_pre, up_pre):
    sigmoid_part = jax.nn.sigmoid(gate_pre)
    gate_back = (
        hidden_grad * up_pre * sigmoid_part * (1.0 + gate_pre * (1.0 - sigmoid_part))
    ).astype(jnp.bfloat16)
    up_back = (hidden_grad * gate_pre * sigmoid_part).astype(jnp.bfloat16)
    return (gate_back, up_back)


def per_device(
    tokens,
    cotangent,
    routes,
    norm_in,
    query_w,
    key_w,
    value_w,
    out_w,
    query_gain,
    key_gain,
    norm_mid,
    router_w,
    gate_w,
    up_w,
    down_w,
):
    rows_own = tokens.shape[0]
    model_width = tokens.shape[1]
    tensor_count = lax.axis_size("tensor")
    expert_count = lax.axis_size("expert")
    head_width = query_gain.shape[0]
    local_heads = query_w.shape[1] // head_width
    experts_local = gate_w.shape[0]
    experts_all = router_w.shape[1]
    top_count = routes.shape[1]
    hidden_width = gate_w.shape[2]
    factor = 1.0 / math.sqrt(head_width)
    cot_all = lax.all_gather(cotangent, "expert", axis=0, tiled=True)
    source = tokens.astype(jnp.float32)
    scale_in = inverse_rms(source)
    normed_low = (source * scale_in * norm_in).astype(jnp.bfloat16)
    gathered = lax.all_gather(normed_low, "tensor", axis=0, tiled=True)
    seq_len = gathered.shape[0]
    query_pre = jnp.dot(gathered, query_w, preferred_element_type=jnp.float32)
    key_pre = jnp.dot(gathered, key_w, preferred_element_type=jnp.float32)
    value_low = jnp.dot(gathered, value_w, preferred_element_type=jnp.float32).astype(jnp.bfloat16)
    cosine, sine_table = rotary_tables(seq_len, head_width)
    query_heads = query_pre.reshape(seq_len, local_heads, head_width)
    key_heads = key_pre.reshape(seq_len, local_heads, head_width)
    query_scale = inverse_rms(query_heads)
    key_scale = inverse_rms(key_heads)
    query_low = rotate(query_heads * query_scale * query_gain, cosine, sine_table).astype(
        jnp.bfloat16
    )
    key_low = rotate(key_heads * key_scale * key_gain, cosine, sine_table).astype(jnp.bfloat16)
    value_heads = value_low.reshape(seq_len, local_heads, head_width)
    block_rows = min(512, seq_len)
    block_count = seq_len // block_rows
    query_blocks = query_low.reshape(block_count, block_rows, local_heads, head_width)

    def attend(query_block):
        scores = (
            jnp.einsum("qhd,khd->hqk", query_block, key_low, preferred_element_type=jnp.float32)
            * factor
        )
        row_max = jnp.max(scores, axis=-1, keepdims=True)
        shifted = jnp.exp(scores - row_max)
        row_sum = jnp.sum(shifted, axis=-1, keepdims=True)
        probs_low = (shifted / row_sum).astype(jnp.bfloat16)
        mixture = jnp.einsum(
            "hqk,khd->qhd", probs_low, value_heads, preferred_element_type=jnp.float32
        )
        return (mixture.astype(jnp.bfloat16), (row_max + jnp.log(row_sum))[..., 0])

    attended_blocks, log_sums = lax.map(attend, query_blocks)
    attended = attended_blocks.reshape(seq_len, local_heads * head_width)
    attn_out = lax.psum_scatter(
        jnp.dot(attended, out_w, preferred_element_type=jnp.float32).astype(jnp.bfloat16),
        "tensor",
        scatter_dimension=0,
        tiled=True,
    ).astype(jnp.float32)
    middle = source + attn_out
    scale_mid = inverse_rms(middle)
    normed_mid = middle * scale_mid * norm_mid
    mid_low = normed_mid.astype(jnp.bfloat16)
    logits = jnp.dot(normed_mid, router_w, precision=highest, preferred_element_type=jnp.float32)
    route_mask = routes[:, :, None] == jnp.arange(experts_all, dtype=jnp.int32)[None, None, :]
    mask_float = route_mask.astype(jnp.float32)
    chosen = jnp.sum(mask_float * logits[:, None, :], axis=-1)
    gating = jax.nn.softmax(chosen, axis=-1)
    upstream = cotangent.astype(jnp.float32)
    gates = jnp.sum(mask_float * gating[:, :, None], axis=1)
    x_all = lax.all_gather(mid_low, "expert", axis=0, tiled=True)
    gates_all = lax.all_gather(gates, "expert", axis=0, tiled=True)
    first_expert = lax.axis_index("expert") * experts_local
    own_gates = lax.dynamic_slice_in_dim(gates_all, first_expert, experts_local, 1)
    part_width = hidden_width // tensor_count
    rows_all = x_all.shape[0]
    y_part = jnp.zeros((rows_all, model_width), jnp.float32)
    x_grad_part = jnp.zeros((rows_all, model_width), jnp.float32)
    gate_grads, gate_parts, up_parts, down_parts = ([], [], [], [])
    for e in range(experts_local):
        hidden_raw = lax.dot_general(
            cot_all, down_w[e], contract_last, preferred_element_type=jnp.float32
        )
        gate_pre = jnp.dot(x_all, gate_w[e], preferred_element_type=jnp.float32)
        up_pre = jnp.dot(x_all, up_w[e], preferred_element_type=jnp.float32)
        weight = own_gates[:, e : e + 1]
        hidden = gate_pre * jax.nn.sigmoid(gate_pre) * up_pre
        gate_grads.append(jnp.sum(hidden * hidden_raw, axis=1))
        hidden_low = (hidden * weight).astype(jnp.bfloat16)
        gate_back, up_back = swiglu_back(hidden_raw * weight, gate_pre, up_pre)
        y_part = y_part + jnp.dot(hidden_low, down_w[e], preferred_element_type=jnp.float32)
        x_grad_part = x_grad_part + lax.dot_general(
            gate_back, gate_w[e], contract_last, preferred_element_type=jnp.float32
        )
        x_grad_part = x_grad_part + lax.dot_general(
            up_back, up_w[e], contract_last, preferred_element_type=jnp.float32
        )
        gate_parts.append(
            jnp.einsum(
                "nd,ntf->tdf",
                x_all,
                gate_back.reshape(rows_all, tensor_count, part_width),
                preferred_element_type=jnp.float32,
            ).astype(jnp.bfloat16)
        )
        up_parts.append(
            jnp.einsum(
                "nd,ntf->tdf",
                x_all,
                up_back.reshape(rows_all, tensor_count, part_width),
                preferred_element_type=jnp.float32,
            ).astype(jnp.bfloat16)
        )
        down_parts.append(
            lax.dot_general(
                hidden_low, cot_all, contract_first, preferred_element_type=jnp.float32
            ).astype(jnp.bfloat16)
        )
    x_grad = lax.psum_scatter(
        x_grad_part.astype(jnp.bfloat16), "expert", scatter_dimension=0, tiled=True
    )
    expert_input_grad = x_grad.astype(jnp.float32)
    gate_grad_sent = jnp.stack(gate_grads, axis=-1)
    gate_grad_all = lax.all_to_all(
        gate_grad_sent, "expert", split_axis=0, concat_axis=0, tiled=True
    )
    gate_grad_dense = (
        gate_grad_all.reshape(expert_count, rows_own, experts_local)
        .transpose(1, 0, 2)
        .reshape(rows_own, experts_all)
    )
    gate_grad = jnp.sum(mask_float * gate_grad_dense[:, None, :], axis=-1)
    y_sum = lax.psum_scatter(y_part.astype(jnp.bfloat16), "expert", scatter_dimension=0, tiled=True)
    output = (middle + y_sum.astype(jnp.float32)).astype(jnp.bfloat16)

    def own_part(parts):
        return [
            lax.psum_scatter(p, "tensor", scatter_dimension=0, tiled=True).astype(jnp.float32)
            for p in parts
        ]

    gate_w_grad = jnp.concatenate(own_part(gate_parts), axis=0)
    up_w_grad = jnp.concatenate(own_part(up_parts), axis=0)
    down_w_grad = jnp.stack(own_part(down_parts), axis=0)
    inner_gate = jnp.sum(gating * gate_grad, axis=-1, keepdims=True)
    chosen_grad = gating * (gate_grad - inner_gate)
    logit_grad = jnp.sum(chosen_grad[:, :, None] * mask_float, axis=1)
    router_part = lax.dot_general(
        normed_mid,
        logit_grad,
        contract_first,
        precision=highest,
        preferred_element_type=jnp.float32,
    )
    normed_mid_grad = expert_input_grad + lax.dot_general(
        logit_grad, router_w, contract_last, precision=highest, preferred_element_type=jnp.float32
    )
    norm_mid_part = jnp.sum(normed_mid_grad * middle * scale_mid, axis=0)
    middle_grad = upstream + norm_backward(normed_mid_grad, middle, scale_mid, norm_mid)
    branch_low = middle_grad.astype(jnp.bfloat16)
    branch_all = lax.all_gather(branch_low, "tensor", axis=0, tiled=True)
    attended_grad = lax.dot_general(
        branch_all, out_w, contract_last, preferred_element_type=jnp.float32
    ).astype(jnp.bfloat16)
    out_w_part = lax.dot_general(
        attended, branch_all, contract_first, preferred_element_type=jnp.float32
    )
    grad_blocks = attended_grad.reshape(block_count, block_rows, local_heads, head_width)

    def attend_back(carry, inputs):
        key_total, value_total = carry
        query_block, grad_block, log_block = inputs
        scores = (
            jnp.einsum("qhd,khd->hqk", query_block, key_low, preferred_element_type=jnp.float32)
            * factor
        )
        probs = jnp.exp(scores - log_block[:, :, None])
        probs_low = probs.astype(jnp.bfloat16)
        value_total = value_total + jnp.einsum(
            "hqk,qhd->khd", probs_low, grad_block, preferred_element_type=jnp.float32
        )
        prob_grad = jnp.einsum(
            "qhd,khd->hqk", grad_block, value_heads, preferred_element_type=jnp.float32
        )
        delta = jnp.sum(probs * prob_grad, axis=-1, keepdims=True)
        score_low = (probs * (prob_grad - delta)).astype(jnp.bfloat16)
        query_part = (
            jnp.einsum("hqk,khd->qhd", score_low, key_low, preferred_element_type=jnp.float32)
            * factor
        )
        key_total = (
            key_total
            + jnp.einsum("hqk,qhd->khd", score_low, query_block, preferred_element_type=jnp.float32)
            * factor
        )
        return ((key_total, value_total), query_part)

    zero_heads = jnp.zeros((seq_len, local_heads, head_width), jnp.float32)
    (key_grad, value_total), query_parts = lax.scan(
        attend_back, (zero_heads, zero_heads), (query_blocks, grad_blocks, log_sums)
    )
    query_grad = query_parts.reshape(seq_len, local_heads, head_width)
    value_grad_low = value_total.reshape(seq_len, local_heads * head_width).astype(jnp.bfloat16)
    query_rot_grad = rotate_back(query_grad, cosine, sine_table)
    key_rot_grad = rotate_back(key_grad, cosine, sine_table)
    query_gain_part = jnp.sum(query_rot_grad * query_heads * query_scale, axis=(0, 1))
    key_gain_part = jnp.sum(key_rot_grad * key_heads * key_scale, axis=(0, 1))
    query_pre_grad = (
        norm_backward(query_rot_grad, query_heads, query_scale, query_gain)
        .reshape(seq_len, local_heads * head_width)
        .astype(jnp.bfloat16)
    )
    key_pre_grad = (
        norm_backward(key_rot_grad, key_heads, key_scale, key_gain)
        .reshape(seq_len, local_heads * head_width)
        .astype(jnp.bfloat16)
    )
    query_w_part = lax.dot_general(
        gathered, query_pre_grad, contract_first, preferred_element_type=jnp.float32
    )
    key_w_part = lax.dot_general(
        gathered, key_pre_grad, contract_first, preferred_element_type=jnp.float32
    )
    value_w_part = lax.dot_general(
        gathered, value_grad_low, contract_first, preferred_element_type=jnp.float32
    )
    summed = lax.dot_general(
        query_pre_grad, query_w, contract_last, preferred_element_type=jnp.float32
    )
    summed = summed + lax.dot_general(
        key_pre_grad, key_w, contract_last, preferred_element_type=jnp.float32
    )
    rows_grad = lax.psum_scatter(
        (
            summed
            + lax.dot_general(
                value_grad_low, value_w, contract_last, preferred_element_type=jnp.float32
            )
        ).astype(jnp.bfloat16),
        "tensor",
        scatter_dimension=0,
        tiled=True,
    ).astype(jnp.float32)
    norm_in_part = jnp.sum(rows_grad * source * scale_in, axis=0)
    input_grad = middle_grad + norm_backward(rows_grad, source, scale_in, norm_in)
    query_w_grad, key_w_grad, value_w_grad, out_w_grad = (
        lax.psum_scatter(
            query_w_part.astype(jnp.bfloat16), "expert", scatter_dimension=0, tiled=True
        ).astype(jnp.float32),
        lax.psum_scatter(
            key_w_part.astype(jnp.bfloat16), "expert", scatter_dimension=0, tiled=True
        ).astype(jnp.float32),
        lax.psum_scatter(
            value_w_part.astype(jnp.bfloat16), "expert", scatter_dimension=0, tiled=True
        ).astype(jnp.float32),
        lax.psum_scatter(
            out_w_part.astype(jnp.bfloat16), "expert", scatter_dimension=1, tiled=True
        ).astype(jnp.float32),
    )
    norm_in_grad, query_gain_grad, key_gain_grad, norm_mid_grad, router_w_grad = lax.psum(
        (norm_in_part, query_gain_part, key_gain_part, norm_mid_part, router_part),
        ("expert", "tensor"),
    )
    return (
        output,
        input_grad,
        norm_in_grad,
        query_w_grad,
        key_w_grad,
        value_w_grad,
        out_w_grad,
        query_gain_grad,
        key_gain_grad,
        norm_mid_grad,
        router_w_grad,
        gate_w_grad,
        up_w_grad,
        down_w_grad,
    )


def solution(mesh):
    placed = (
        P(("expert", "tensor"), None),
        P(("expert", "tensor"), None),
        P(("expert", "tensor"), None),
        P(),
        P(None, "tensor"),
        P(None, "tensor"),
        P(None, "tensor"),
        P("tensor", None),
        P(),
        P(),
        P(),
        P(),
        P("expert", None, None),
        P("expert", None, None),
        P("expert", None, None),
    )
    return jax.shard_map(
        per_device,
        mesh=mesh,
        in_specs=placed,
        out_specs=(
            P(("expert", "tensor"), None),
            P(("expert", "tensor"), None),
            P(),
            P("expert", "tensor"),
            P("expert", "tensor"),
            P("expert", "tensor"),
            P("tensor", "expert"),
            P(),
            P(),
            P(),
            P(),
            P("expert", None, "tensor"),
            P("expert", None, "tensor"),
            P("expert", "tensor", None),
        ),
        check_vma=False,
    )
```

profile of v0, /device:TPU:0, one launch (start us, length us, event | category | flops | bytes accessed | tf_op | source)
XLA Modules:
  0.0 1698.5 jit_solution(10612123125915313644)
XLA Ops:
  14.0 35.3 %all-gather.5.cloned.1.call-done = bf16[1024,2048]{1,0:T(8,128)(2,1)} async-done(((bf16[256,2048]{1,0:T(8,128)(2,1)}), bf16[1024,2048]{1,0:T(8,128)(2,1)}) %all-gather.5.cloned.1.call-update) | async-done | bytes 4194320 | tf_op jit(solution)/shard_map/all_gather | solution.py:99
  106.5 44.6 %reduce-scatter.15.cloned.1.call-done = bf16[256,2048]{1,0:T(8,128)(2,1)} async-done(((bf16[1024,2048]{1,0:T(8,128)(2,1)}), bf16[256,2048]{1,0:T(8,128)(2,1)}) %reduce-scatter.15.cloned.1.call-update) | async-done | bytes 1048592 | tf_op jit(solution)/shard_map/reduce_scatter | solution.py:134
  156.0 124.5 %all-gather.7.cloned.1.call-done = bf16[2048,2048]{1,0:T(8,128)(2,1)} async-done(((bf16[256,2048]{1,0:T(8,128)(2,1)}), bf16[2048,2048]{1,0:T(8,128)(2,1)}) %all-gather.7.cloned.1.call-update) | async-done | bytes 8388624 | tf_op jit(solution)/shard_map/all_gather | solution.py:151
  308.6 97.2 %all-gather.9.cloned.1.call-done = bf16[2048,2048]{1,0:T(8,128)(2,1)} async-done(((bf16[256,2048]{1,0:T(8,128)(2,1)}), bf16[2048,2048]{1,0:T(8,128)(2,1)}) %all-gather.9.cloned.1.call-update) | async-done | bytes 8388624 | tf_op jit(solution)/shard_map/all_gather | solution.py:95
  405.8 20.0 %multiply_reduce_fusion.3 = (f32[2048]{0:T(1024)S(1)}, f32[2048,1024]{0,1:T(8,128)}) fusion(f32[2048,1024]{0,1:T(8,128)} %fusion.51, f32[2048,1024]{0,1:T(8,128)} %fusion.55, bf16[2048,2048]{1,0:T(8,128)(2,1)} %all-gather.9.cloned.1.call-done, bf16[2,1024,2048]{2,1,0:T(8,128)(2,1)} %param.33), kind=kOutput, calls=%fused_computation.50 | convolution fusion | flops 8604612608 | bytes 37756928 | tf_op jit(solution)/shard_map/dot_general | solution.py:161
  438.4 17.6 %fusion.43 = f32[2048,1024]{0,1:T(8,128)} fusion(bf16[2048,2048]{1,0:T(8,128)(2,1)} %all-gather.7.cloned.1.call-done, bf16[2,2048,1024]{2,1,0:T(8,128)(2,1)} %param.31), kind=kOutput, calls=%fused_computation.79 | convolution fusion | flops 8589934592 | bytes 20971520 | tf_op jit(solution)/shard_map/dot_general | solution.py:164
  456.0 17.1 %multiply_reduce_fusion.2 = (f32[2048]{0:T(1024)S(1)}, f32[2048,1024]{0,1:T(8,128)}) fusion(f32[2048,1024]{0,1:T(8,128)S(1)} %fusion.39, f32[2048,1024]{0,1:T(8,128)} %fusion.43, bf16[2048,2048]{1,0:T(8,128)(2,1)} %all-gather.9.cloned.1.call-done, bf16[2,1024,2048]{2,1,0:T(8,128)(2,1)} %param.33), kind=kOutput, calls=%fused_computation.49 | convolution fusion | flops 8604612608 | bytes 37756928 | tf_op jit(solution)/shard_map/dot_general | solution.py:161
  483.8 30.6 %all_gather.17 = f32[2048,16]{0,1:T(8,128)S(1)} all-gather(f32[256,16]{0,1:T(8,128)S(1)} %get-tuple-element.252), channel_id=1, replica_groups=mesh['expert'=8,'tensor'=4] {'expert'}, dimensions={0}, use_global_device_ids=true | all-gather | bytes 147456 | tf_op jit(solution)/shard_map/all_gather | solution.py:152
  551.8 16.7 fusion.53
  582.6 25.5 %add_convert_fusion = bf16[2048,2048]{1,0:T(8,128)(2,1)} fusion(f32[2048,2048]{1,0:T(8,128)} %fusion.41, f32[2048,2048]{1,0:T(8,128)} %fusion.53, f32[2048,2048]{1,0:T(8,128)} %fusion.49, bf16[2048,1024]{0,1:T(8,128)(2,1)} %get-tuple-element.299, bf16[2,2048,1024]{2,1,0:T(8,128)(2,1)} %param.32), kind=kOutput, calls=%fused_computation.38 | convolution fusion | flops 8606711808 | bytes 67108864 | tf_op jit(solution)/shard_map/dot_general | solution.py:175
  608.2 147.1 %reduce-scatter.19.cloned.1.call-done = bf16[256,2048]{1,0:T(8,128)(2,1)} async-done(((bf16[2048,2048]{1,0:T(8,128)(2,1)}), bf16[256,2048]{1,0:T(8,128)(2,1)}) %reduce-scatter.19.cloned.1.call-update) | async-done | bytes 1048592 | tf_op jit(solution)/shard_map/reduce_scatter | solution.py:199
  820.9 16.9 convolution_convert_fusion
  868.4 30.6 %while.28 = (s32[]{:T(128)}, f32[1024,4,128]{0,2,1:T(8,128)}, f32[1024,4,128]{0,2,1:T(8,128)}, f32[2,512,4,128]{3,1,0,2:T(8,128)}, bf16[2,512,4,128]{3,1,2,0:T(8...) while((s32[]{:T(128)}, f32[1024,4,128]{0,2,1:T(8,128)}, ...), condition=%wide.region_23.24_spmd.clone, body=%wide.region_21.23_spmd.clone.sunk | while | flops 2712401920 | bytes 137421200 | solution.py:279
  960.5 20.5 %fusion.47 = f32[2048,2048]{1,0:T(8,128)} fusion(bf16[2,1024,2048]{2,1,0:T(8,128)(2,1)} %param.33, f32[2048]{0:T(1024)S(1)} %bitcast.295, f32[2048,1024]{0,1:T(8,128)} %fusion.51, f32[2048,1024]{0,1:T(8,128)} %fusion.55), kind=kOutput, calls=%fused_computation.83 | convolution fusion | flops 8604614656 | bytes 37756928 | tf_op jit(solution)/shard_map/dot_general | solution.py:171
  980.9 21.9 %add_convert_fusion.1 = bf16[2048,2048]{1,0:T(8,128)(2,1)} fusion(f32[2048,2048]{1,0:T(8,128)} %fusion.47, bf16[2,1024,2048]{2,1,0:T(8,128)(2,1)} %param.33, f32[2048]{0:T(1024)S(1)} %bitcast.292, f32[2048,1024]{0,1:T(8,128)} %copy-done.15, f32[2048,1024]{0,1:T(8,128)} %fusion.43), kind=kOutput, calls=%fused_computation.39 | convolution fusion | flops 8613003264 | bytes 46145536 | tf_op jit(solution)/shard_map/dot_general | solution.py:171
  1034.2 47.1 %reduce-scatter.39.cloned.1.call-done = bf16[256,2048]{1,0:T(8,128)(2,1)} async-done(((bf16[1024,2048]{1,0:T(8,128)(2,1)}), bf16[256,2048]{1,0:T(8,128)(2,1)}) %reduce-scatter.39.cloned.1.call-update) | async-done | bytes 1048592 | tf_op jit(solution)/shard_map/reduce_scatter | solution.py:218
  1085.1 68.0 %reduce-scatter.29.cloned.1.call-done = bf16[512,256]{1,0:T(8,128)(2,1)} async-done(((bf16[512,2048]{1,0:T(8,128)(2,1)}), bf16[512,256]{1,0:T(8,128)(2,1)}) %reduce-scatter.29.cloned.1.call-update) | async-done | bytes 262160 | tf_op jit(solution)/shard_map/reduce_scatter | solution.py:336
  1154.9 68.2 %reduce-scatter.27.cloned.1.call-done = bf16[256,512]{1,0:T(8,128)(2,1)} async-done(((bf16[2048,512]{1,0:T(8,128)(2,1)}), bf16[256,512]{1,0:T(8,128)(2,1)}) %reduce-scatter.27.cloned.1.call-update) | async-done | bytes 262160 | tf_op jit(solution)/shard_map/reduce_scatter | solution.py:333
  1224.8 68.2 %reduce-scatter.23.cloned.1.call-done = bf16[256,512]{1,0:T(8,128)(2,1)} async-done(((bf16[2048,512]{1,0:T(8,128)(2,1)}), bf16[256,512]{1,0:T(8,128)(2,1)}) %reduce-scatter.23.cloned.1.call-update) | async-done | bytes 262160 | tf_op jit(solution)/shard_map/reduce_scatter | solution.py:327
  1294.8 68.9 %reduce-scatter.25.cloned.1.call-done = bf16[256,512]{1,0:T(8,128)(2,1)} async-done(((bf16[2048,512]{1,0:T(8,128)(2,1)}), bf16[256,512]{1,0:T(8,128)(2,1)}) %reduce-scatter.25.cloned.1.call-update) | async-done | bytes 262160 | tf_op jit(solution)/shard_map/reduce_scatter | solution.py:330
  1365.5 44.1 %reduce-scatter.21.cloned.1.call-done = bf16[256,2048]{1,0:T(8,128)(2,1)} async-done(((bf16[1024,2048]{1,0:T(8,128)(2,1)}), bf16[256,2048]{1,0:T(8,128)(2,1)}) %reduce-scatter.21.cloned.1.call-update) | async-done | bytes 1048592 | tf_op jit(solution)/shard_map/reduce_scatter | solution.py:313
  1411.5 151.1 %reduce-scatter.17.cloned.1.call-done = bf16[256,2048]{1,0:T(8,128)(2,1)} async-done(((bf16[2048,2048]{1,0:T(8,128)(2,1)}), bf16[256,2048]{1,0:T(8,128)(2,1)}) %reduce-scatter.17.cloned.1.call-update) | async-done | bytes 1048592 | tf_op jit(solution)/shard_map/reduce_scatter | solution.py:213
  1568.9 39.5 %all-reduce = (f32[2048]{0:T(1024)}, f32[128]{0:T(128)}, f32[128]{0:T(128)}, f32[2048]{0:T(1024)}) all-reduce(f32[2048]{0:T(1024)S(1)} %get-tuple-element.249, f32[128]{0:T(128)S(1)} %bitcast_reduce_fusion.1, f32[128]{0:T(128)S(1)} %bitcast_reduce_fusion, ...), channel_id=1, replica_groups=mesh['expert'=8,'tensor'=4] {'expert','tensor'}, use_global_device_ids=true, to_apply=%region_29.30 | all-reduce | flops 4352 | bytes 34816 | tf_op jit(solution)/shard_map/psum | solution.py:340
  1608.5 81.7 %all-reduce.3.cloned.1.call-done = f32[2048,16]{0,1:T(8,128)} async-done(((f32[2048,16]{0,1:T(8,128)}), f32[2048,16]{0,1:T(8,128)}) %all-reduce.3.cloned.1.call-update) | async-done | bytes 131088 | tf_op jit(solution)/shard_map/psum | solution.py:340
  (317 shorter events, 427.0 us)
Async XLA Ops:
  7.2 42.1 %all-gather.5.cloned.1.call-start = ((), (), s32[]{:S(2)}) async-start(), calls=%async_computation.15 | async-start | bytes 5242880 | tf_op jit(solution)/shard_map/all_gather | solution.py:99
  12.0 139.1 %reduce-scatter.15.cloned.1.call-start = ((), (), s32[]{:S(2)}) async-start(), calls=%async_computation.16 | async-start | bytes 5242880 | tf_op jit(solution)/shard_map/reduce_scatter | solution.py:134
  106.4 174.0 %all-gather.7.cloned.1.call-start = ((), (), s32[]{:S(2)}) async-start(), calls=%async_computation.17 | async-start | bytes 9437184 | tf_op jit(solution)/shard_map/all_gather | solution.py:151
  152.8 607.5 %copy-start.44 = (f32[256]{0:T(256)}, f32[256]{0:T(256)S(1)}, u32[]{:S(2)}) copy-start(f32[256]{0:T(256)S(1)} %add_rsqrt_fusion.2) | copy-start | bytes 3076
  155.4 250.4 %all-gather.9.cloned.1.call-start = ((), (), s32[]{:S(2)}) async-start(), calls=%async_computation.19 | async-start | bytes 9437184 | tf_op jit(solution)/shard_map/all_gather | solution.py:95
  473.7 9.9 all-to-all-start
  477.0 278.3 %reduce-scatter.19.cloned.1.call-start = ((), (), s32[]{:S(2)}) async-start(), calls=%async_computation.20 | async-start | bytes 9437184 | tf_op jit(solution)/shard_map/reduce_scatter | solution.py:199
  608.2 246.3 %all-gather.11.cloned.1.call-start = ((), (), s32[]{:S(2)}) async-start(), calls=%async_computation.21 | async-start | bytes 5242880 | tf_op jit(solution)/shard_map/all_gather | solution.py:241
  763.8 243.8 %reduce-scatter.33.cloned.1.call-start = ((), (), s32[]{:S(2)}) async-start(), calls=%async_computation.29 | async-start | bytes 5242880 | tf_op jit(solution)/shard_map/reduce_scatter | solution.py:218
  777.7 229.9 %reduce-scatter.31.cloned.1.call-start = ((), (), s32[]{:S(2)}) async-start(), calls=%async_computation.28 | async-start | bytes 5242880 | tf_op jit(solution)/shard_map/reduce_scatter | solution.py:218
  791.8 225.4 %reduce-scatter.37.cloned.1.call-start = ((), (), s32[]{:S(2)}) async-start(), calls=%async_computation.31 | async-start | bytes 5242880 | tf_op jit(solution)/shard_map/reduce_scatter | solution.py:218
  805.8 211.5 %reduce-scatter.35.cloned.1.call-start = ((), (), s32[]{:S(2)}) async-start(), calls=%async_computation.30 | async-start | bytes 5242880 | tf_op jit(solution)/shard_map/reduce_scatter | solution.py:218
  820.9 213.3 %reduce-scatter.41.cloned.1.call-start = ((), (), s32[]{:S(2)}) async-start(), calls=%async_computation.33 | async-start | bytes 5242880 | tf_op jit(solution)/shard_map/reduce_scatter | solution.py:218
  837.8 243.4 %reduce-scatter.39.cloned.1.call-start = ((), (), s32[]{:S(2)}) async-start(), calls=%async_computation.32 | async-start | bytes 5242880 | tf_op jit(solution)/shard_map/reduce_scatter | solution.py:218
  854.4 298.7 %reduce-scatter.29.cloned.1.call-start = ((), (), s32[]{:S(2)}) async-start(), calls=%async_computation.26 | async-start | bytes 2359296 | tf_op jit(solution)/shard_map/reduce_scatter | solution.py:336
  868.3 354.7 %reduce-scatter.27.cloned.1.call-start = ((), (), s32[]{:S(2)}) async-start(), calls=%async_computation.25 | async-start | bytes 2359296 | tf_op jit(solution)/shard_map/reduce_scatter | solution.py:333
  908.3 384.7 %reduce-scatter.23.cloned.1.call-start = ((), (), s32[]{:S(2)}) async-start(), calls=%async_computation.23 | async-start | bytes 2359296 | tf_op jit(solution)/shard_map/reduce_scatter | solution.py:327
  931.8 431.9 %reduce-scatter.25.cloned.1.call-start = ((), (), s32[]{:S(2)}) async-start(), calls=%async_computation.24 | async-start | bytes 2359296 | tf_op jit(solution)/shard_map/reduce_scatter | solution.py:330
  948.0 461.6 %reduce-scatter.21.cloned.1.call-start = ((), (), s32[]{:S(2)}) async-start(), calls=%async_computation.22 | async-start | bytes 5242880 | tf_op jit(solution)/shard_map/reduce_scatter | solution.py:313
  959.8 602.8 %reduce-scatter.17.cloned.1.call-start = ((), (), s32[]{:S(2)}) async-start(), calls=%async_computation.18 | async-start | bytes 9437184 | tf_op jit(solution)/shard_map/reduce_scatter | solution.py:213
  1002.9 687.3 %all-reduce.3.cloned.1.call-start = ((), (), s32[]{:S(2)}) async-start(), calls=%async_computation.27 | async-start | bytes 262144 | tf_op jit(solution)/shard_map/psum | solution.py:340
  1081.3 328.4 %copy-start.34 = (f32[2048]{0:T(1024)S(1)}, f32[2048]{0:T(1024)}, u32[]{:S(2)}) copy-start(f32[2048]{0:T(1024)} %param.22) | copy-start | bytes 24580
  1081.3 328.4 %copy-start.43 = (f32[256]{0:T(256)S(1)}, f32[256]{0:T(256)}, u32[]{:S(2)}) copy-start(f32[256]{0:T(256)} %copy-done.42) | copy-start | bytes 3076
  1085.1 477.5 %copy-start.49 = (f32[256]{0:T(256)S(1)}, f32[256]{0:T(256)}, u32[]{:S(2)}) copy-start(f32[256]{0:T(256)} %copy-done.48) | copy-start | bytes 3076
  (71 other events, 1674.2 us)
Sparse Core Ops, SparseCore 0:
  12.1 37.1 all-gather.4
  106.5 44.5 reduce-scatter.14
  155.5 124.8 all-gather.6
  282.6 123.1 all-gather.8
  608.3 147.0 reduce-scatter.18
  763.9 33.4 all-gather.10
  799.9 44.5 reduce-scatter.32
  847.7 44.5 reduce-scatter.30
  895.4 44.5 reduce-scatter.36
  942.5 44.5 reduce-scatter.34
  989.6 44.5 reduce-scatter.40
  1036.7 44.5 reduce-scatter.38
  1084.8 68.2 reduce-scatter.28
  1156.5 66.5 reduce-scatter.26
  1226.4 66.5 reduce-scatter.22
  1297.0 66.6 reduce-scatter.24
  1366.1 43.4 reduce-scatter.20
  1413.5 149.0 reduce-scatter.16
  1568.7 121.4 all-reduce.2
where the time goes:
time: 1700 us
  waiting for transfers between devices  1060 us (62%)
  matrix products  404 us (24%)
  other arithmetic  99.1 us (6%)
  blocking collectives  70.1 us (4%)
  local copies, waits for them, and re-layouts  46.5 us (3%)
    reduce_scatter x1, waiting for transfers between devices, per_device(): lax.psum_scatter(y_part.astype(jnp.bfloat16), 'expert', scatter_dimension...  151 us
    reduce_scatter x1, waiting for transfers between devices, per_device(): lax.psum_scatter(x_grad_part.astype(jnp.bfloat16), 'expert', scatter_dime...  147 us
    all_gather x1, waiting for transfers between devices, per_device(): x_all = lax.all_gather(mid_low, 'expert', axis=0, tiled=True)  124 us
    all_gather x1, waiting for transfers between devices, per_device(): cot_all = lax.all_gather(cotangent, 'expert', axis=0, tiled=True)  97.2 us
    psum x1, waiting for transfers between devices, per_device(): lax.psum((norm_in_part, query_gain_part, key_gain_part, norm_mid_part, ro...  81.7 us
    reduce_scatter x1, waiting for transfers between devices, per_device(): lax.psum_scatter(key_w_part.astype(jnp.bfloat16), 'expert', scatter_dimen...  68.9 us
    reduce_scatter x1, waiting for transfers between devices, per_device(): lax.psum_scatter(query_w_part.astype(jnp.bfloat16), 'expert', scatter_dim...  68.2 us
    reduce_scatter x1, waiting for transfers between devices, per_device(): lax.psum_scatter(value_w_part.astype(jnp.bfloat16), 'expert', scatter_dim...  68.2 us
  transfers between devices with their start and end apart: 20, of which 15 were waited for; matrix products, arithmetic and copies ran while one was open for 18% of the time, Pallas kernels for 0%

commit v1 on v0

--- a/solution.py
+++ b/solution.py
@@ -1,3 +1,4 @@
+import functools
 import math
 import jax
 import jax.numpy as jnp
@@ -8,6 +9,39 @@
 highest = lax.Precision.HIGHEST
 contract_last = (((1,), (1,)), ((), ()))
 contract_first = (((0,), (0,)), ((), ()))
+
+
+def convert_leaf_over_axis(incoming_x, axis_k):
+    incoming_x = jnp.moveaxis(incoming_x, 0, axis_k)
+    state_now = incoming_x.shape
+    return incoming_x.reshape(
+        *state_now[:axis_k], state_now[axis_k] * state_now[axis_k + 1], *state_now[axis_k + 2 :]
+    )
+
+
+def switch_the_keys(packet, named_axis, ndim_at):
+    q_n = lax.axis_size(named_axis)
+    nodes = []
+    for s in [*range(q_n)]:
+        nodes.append((s, (s + 1) % q_n))
+    panels = []
+    for dev_i, t in nodes:
+        panels.append((t, dev_i))
+    arr_out, current_arr = ([], [])
+    for nth in tuple(range(q_n - 1)):
+        if nth % 2 == 0:
+            arr_out.append(lax.ppermute(arr_out[-1] if arr_out else packet, named_axis, perm=nodes))
+        else:
+            current_arr.append(
+                lax.ppermute(current_arr[-1] if current_arr else packet, named_axis, perm=panels)
+            )
+    arr_next = jnp.stack([*arr_out[::-1], packet, *current_arr])
+    field_out = lax.axis_index(named_axis) - len(arr_out)
+    arr_next = arr_next[(jnp.arange(q_n) - field_out) % q_n]
+    return convert_leaf_over_axis(arr_next, ndim_at)
+
+
+samples_scan = functools.partial(switch_the_keys, named_axis="expert", ndim_at=0)
 
 
 def inverse_rms(values):
@@ -148,7 +182,7 @@
     gating = jax.nn.softmax(chosen, axis=-1)
     upstream = cotangent.astype(jnp.float32)
     gates = jnp.sum(mask_float * gating[:, :, None], axis=1)
-    x_all = lax.all_gather(mid_low, "expert", axis=0, tiled=True)
+    x_all = samples_scan(mid_low)
     gates_all = lax.all_gather(gates, "expert", axis=0, tiled=True)
     first_expert = lax.axis_index("expert") * experts_local
     own_gates = lax.dynamic_slice_in_dim(gates_all, first_expert, experts_local, 1)

time: 1700 us -> 1610 us (0.947)
  waiting for transfers between devices: 1060 us -> 907 us
  starting transfers between devices: 4.91 us -> 35.2 us
  local copies, waits for them, and re-layouts: 46.5 us -> 72.2 us
    ppermute x0 -> x7, waiting for transfers between devices: none -> 155 us  [the longest x4 155 us: switch_the_keys(): lax.ppermute(arr_out[-1] if arr_out else packet, named_axis, perm=nodes)]
    all_gather x1 -> x0, waiting for transfers between devices: 124 us -> none  [per_device(): x_all = lax.all_gather(mid_low, 'expert', axis=0, tiled=True)]
    all_gather x1, waiting for transfers between devices: 97.2 us -> 0.01 us  [per_device(): cot_all = lax.all_gather(cotangent, 'expert', axis=0, tiled=True)]
    psum x1, waiting for transfers between devices: 81.7 us -> 0.01 us  [per_device(): lax.psum((norm_in_part, query_gain_part, key_gain_part, norm_mid_part, ro...]
    ppermute x0 -> x7, starting transfers between devices: none -> 30.1 us  [the longest x3 23.5 us: switch_the_keys(): lax.ppermute(current_arr[-1] if current_arr else packet, named_axis, perm...]
  transfers between devices with their start and end apart: 20 -> 26, of which waited for: 15 -> 16; matrix products, arithmetic and copies ran while one was open for 18% -> 22% of each run, Pallas kernels for 0% -> 0%
where the time goes in v1:
time: 1610 us; the launch traced here: 1600 us
  waiting for transfers between devices  907 us (56%)
  matrix products  404 us (25%)
  other arithmetic  99.1 us (6%)
  local copies, waits for them, and re-layouts  72.2 us (4%)
  blocking collectives  70 us (4%)
  starting transfers between devices  35.2 us (2%)
  between operations  16.4 us (1%)
    ppermute x4, waiting for transfers between devices, switch_the_keys(): lax.ppermute(arr_out[-1] if arr_out else packet, named_axis, perm=nodes)  155 us
    reduce_scatter x1, waiting for transfers between devices, per_device(): lax.psum_scatter(y_part.astype(jnp.bfloat16), 'expert', scatter_dimension...  151 us
    reduce_scatter x1, waiting for transfers between devices, per_device(): lax.psum_scatter(x_grad_part.astype(jnp.bfloat16), 'expert', scatter_dime...  144 us
    reduce_scatter x1, waiting for transfers between devices, per_device(): lax.psum_scatter(key_w_part.astype(jnp.bfloat16), 'expert', scatter_dimen...  69.1 us
    reduce_scatter x1, waiting for transfers between devices, per_device(): lax.psum_scatter(value_w_part.astype(jnp.bfloat16), 'expert', scatter_dim...  68.5 us
    reduce_scatter x1, waiting for transfers between devices, per_device(): lax.psum_scatter(query_w_part.astype(jnp.bfloat16), 'expert', scatter_dim...  68.4 us
    reduce_scatter x1, waiting for transfers between devices, per_device(): lax.psum_scatter(out_w_part.astype(jnp.bfloat16), 'expert', scatter_dimen...  67.8 us
    reduce_scatter x6, waiting for transfers between devices, own_part(): lax.psum_scatter(p, 'tensor', scatter_dimension=0, tiled=True)  54.9 us
  transfers between devices with their start and end apart: 26, of which 16 were waited for; matrix products, arithmetic and copies ran while one was open for 22% of the time, Pallas kernels for 0%

profile of v1, /device:TPU:0, one launch (start us, length us, event | category | flops | bytes accessed | tf_op | source)
XLA Modules:
  0.0 1604.5 jit_solution(2677052904935464488)
XLA Ops:
  14.9 35.3 %all-gather.4.cloned.1.call-done = bf16[1024,2048]{1,0:T(8,128)(2,1)} async-done(((bf16[256,2048]{1,0:T(8,128)(2,1)}), bf16[1024,2048]{1,0:T(8,128)(2,1)}) %all-gather.4.cloned.1.call-update) | async-done | bytes 4194320 | tf_op jit(solution)/shard_map/all_gather | solution.py:133
  107.3 44.6 %reduce-scatter.15.cloned.1.call-done = bf16[256,2048]{1,0:T(8,128)(2,1)} async-done(((bf16[1024,2048]{1,0:T(8,128)(2,1)}), bf16[256,2048]{1,0:T(8,128)(2,1)}) %reduce-scatter.15.cloned.1.call-update) | async-done | bytes 1048592 | tf_op jit(solution)/shard_map/reduce_scatter | solution.py:168
  157.7 26.3 %collective-permute-done = bf16[256,2048]{1,0:T(8,128)(2,1)S(1)} collective-permute-done((bf16[256,2048]{1,0:T(8,128)(2,1)}, bf16[256,2048]{1,0:T(8,128)(2,1)S(1)}, u32[]{:S(2)}, u32[]{:S(2)}) %collective-permute-start) | collective-permute-done | bytes 1048608 | tf_op jit(solution)/shard_map/ppermute | solution.py:33
  189.7 39.6 %collective-permute-done.1 = bf16[256,2048]{1,0:T(8,128)(2,1)} collective-permute-done((bf16[256,2048]{1,0:T(8,128)(2,1)S(1)}, bf16[256,2048]{1,0:T(8,128)(2,1)}, u32[]{:S(2)}, u32[]{:S(2)}) %collective-permute-start.1) | collective-permute-done | bytes 1048608 | tf_op jit(solution)/shard_map/ppermute | solution.py:33
  246.6 40.1 %collective-permute-done.2 = bf16[256,2048]{1,0:T(8,128)(2,1)} collective-permute-done((bf16[256,2048]{1,0:T(8,128)(2,1)}, bf16[256,2048]{1,0:T(8,128)(2,1)}, u32[]{:S(2)}, u32[]{:S(2)}) %collective-permute-start.2) | collective-permute-done | bytes 1048608 | tf_op jit(solution)/shard_map/ppermute | solution.py:33
  293.3 49.3 %collective-permute-done.3 = bf16[256,2048]{1,0:T(8,128)(2,1)} collective-permute-done((bf16[256,2048]{1,0:T(8,128)(2,1)}, bf16[256,2048]{1,0:T(8,128)(2,1)}, u32[]{:S(2)}, u32[]{:S(2)}) %collective-permute-start.3) | collective-permute-done | bytes 1048608 | tf_op jit(solution)/shard_map/ppermute | solution.py:33
  422.3 19.7 %multiply_reduce_fusion.3 = (f32[2048]{0:T(1024)S(1)}, f32[2048,1024]{0,1:T(8,128)}) fusion(f32[2048,1024]{0,1:T(8,128)} %fusion.43, f32[2048,1024]{0,1:T(8,128)} %fusion.47, bf16[2048,2048]{1,0:T(8,128)(2,1)} %all-gather.6.cloned.1.call-done, bf16[2,1024,2048]{2,1,0:T(8,128)(2,1)} %param.33), kind=kOutput, calls=%fused_computation.43 | convolution fusion | flops 8604612608 | bytes 37756928 | tf_op jit(solution)/shard_map/dot_general | solution.py:195
  442.0 19.6 %multiply_reduce_fusion.2 = (f32[2048]{0:T(1024)S(1)}, f32[2048,1024]{0,1:T(8,128)}) fusion(f32[2048,1024]{0,1:T(8,128)} %fusion.31, f32[2048,1024]{0,1:T(8,128)} %fusion.35, bf16[2048,2048]{1,0:T(8,128)(2,1)} %all-gather.6.cloned.1.call-done, bf16[2,1024,2048]{2,1,0:T(8,128)(2,1)} %param.33), kind=kOutput, calls=%fused_computation.42 | convolution fusion | flops 8604612608 | bytes 37756928 | tf_op jit(solution)/shard_map/dot_general | solution.py:195
  472.5 30.5 %all_gather.13 = f32[2048,16]{0,1:T(8,128)S(1)} all-gather(f32[256,16]{0,1:T(8,128)S(1)} %get-tuple-element.252), channel_id=1, replica_groups=mesh['expert'=8,'tensor'=4] {'expert'}, dimensions={0}, use_global_device_ids=true | all-gather | bytes 147456 | tf_op jit(solution)/shard_map/all_gather | solution.py:186
  540.6 16.9 %fusion.45 = f32[2048,2048]{1,0:T(8,128)} fusion(bf16[2048,1024]{0,1:T(8,128)(2,1)} %get-tuple-element.302, bf16[2,2048,1024]{2,1,0:T(8,128)(2,1)} %param.31), kind=kOutput, calls=%fused_computation.82 | convolution fusion | flops 8589934592 | bytes 25165824 | tf_op jit(solution)/shard_map/dot_general | solution.py:206
  571.7 25.4 %add_convert_fusion = bf16[2048,2048]{1,0:T(8,128)(2,1)} fusion(f32[2048,2048]{1,0:T(8,128)} %fusion.33, f32[2048,2048]{1,0:T(8,128)} %fusion.45, f32[2048,2048]{1,0:T(8,128)} %fusion.41, bf16[2048,1024]{0,1:T(8,128)(2,1)} %get-tuple-element.299, bf16[2,2048,1024]{2,1,0:T(8,128)(2,1)} %param.32), kind=kOutput, calls=%fused_computation.39 | convolution fusion | flops 8606711808 | bytes 67108864 | tf_op jit(solution)/shard_map/dot_general | solution.py:209
  597.2 144.3 %reduce-scatter.19.cloned.1.call-done = bf16[256,2048]{1,0:T(8,128)(2,1)} async-done(((bf16[2048,2048]{1,0:T(8,128)(2,1)}), bf16[256,2048]{1,0:T(8,128)(2,1)}) %reduce-scatter.19.cloned.1.call-update) | async-done | bytes 1048592 | tf_op jit(solution)/shard_map/reduce_scatter | solution.py:233
  807.0 16.9 %convolution_convert_fusion = bf16[1024,2048]{1,0:T(8,128)(2,1)} fusion(bf16[2048,2048]{1,0:T(8,128)(2,1)} %all-gather.6.cloned.1.call-done, f32[2048]{0:T(1024)S(1)} %bitcast.307, f32[2048,1024]{0,1:T(8,128)} %fusion.31, f32[2048,1024]{0,1:T(8,128)} %fusion.35), kind=kOutput, calls=%fused_computation.95 | convolution fusion | flops 8606711808 | bytes 29368320 | tf_op jit(solution)/shard_map/dot_general | solution.py:229
  854.5 30.6 %while.28 = (s32[]{:T(128)}, f32[1024,4,128]{0,2,1:T(8,128)}, f32[1024,4,128]{0,2,1:T(8,128)}, f32[2,512,4,128]{3,1,0,2:T(8,128)}, bf16[2,512,4,128]{3,1,2,0:T(8...) while((s32[]{:T(128)}, f32[1024,4,128]{0,2,1:T(8,128)}, ...), condition=%wide.region_23.24_spmd.clone, body=%wide.region_21.23_spmd.clone.sunk | while | flops 2712401920 | bytes 137421200 | solution.py:313
  947.2 20.2 %fusion.39 = f32[2048,2048]{1,0:T(8,128)} fusion(bf16[2,1024,2048]{2,1,0:T(8,128)(2,1)} %param.33, f32[2048]{0:T(1024)S(1)} %bitcast.311, f32[2048,1024]{0,1:T(8,128)} %fusion.43, f32[2048,1024]{0,1:T(8,128)} %fusion.47), kind=kOutput, calls=%fused_computation.76 | convolution fusion | flops 8604614656 | bytes 37756928 | tf_op jit(solution)/shard_map/dot_general | solution.py:205
  967.4 21.8 %add_convert_fusion.1 = bf16[2048,2048]{1,0:T(8,128)(2,1)} fusion(f32[2048,2048]{1,0:T(8,128)} %fusion.39, bf16[2,1024,2048]{2,1,0:T(8,128)(2,1)} %param.33, f32[2048]{0:T(1024)S(1)} %bitcast.308, f32[2048,1024]{0,1:T(8,128)} %fusion.31, f32[2048,1024]{0,1:T(8,128)} %fusion.35), kind=kOutput, calls=%fused_computation.40 | convolution fusion | flops 8613003264 | bytes 46145536 | tf_op jit(solution)/shard_map/dot_general | solution.py:205
  1020.2 47.3 %reduce-scatter.39.cloned.1.call-done = bf16[256,2048]{1,0:T(8,128)(2,1)} async-done(((bf16[1024,2048]{1,0:T(8,128)(2,1)}), bf16[256,2048]{1,0:T(8,128)(2,1)}) %reduce-scatter.39.cloned.1.call-update) | async-done | bytes 1048592 | tf_op jit(solution)/shard_map/reduce_scatter | solution.py:252
  1071.4 67.8 %reduce-scatter.29.cloned.1.call-done = bf16[512,256]{1,0:T(8,128)(2,1)} async-done(((bf16[512,2048]{1,0:T(8,128)(2,1)}), bf16[512,256]{1,0:T(8,128)(2,1)}) %reduce-scatter.29.cloned.1.call-update) | async-done | bytes 262160 | tf_op jit(solution)/shard_map/reduce_scatter | solution.py:370
  1141.0 68.5 %reduce-scatter.27.cloned.1.call-done = bf16[256,512]{1,0:T(8,128)(2,1)} async-done(((bf16[2048,512]{1,0:T(8,128)(2,1)}), bf16[256,512]{1,0:T(8,128)(2,1)}) %reduce-scatter.27.cloned.1.call-update) | async-done | bytes 262160 | tf_op jit(solution)/shard_map/reduce_scatter | solution.py:367
  1211.3 68.4 %reduce-scatter.23.cloned.1.call-done = bf16[256,512]{1,0:T(8,128)(2,1)} async-done(((bf16[2048,512]{1,0:T(8,128)(2,1)}), bf16[256,512]{1,0:T(8,128)(2,1)}) %reduce-scatter.23.cloned.1.call-update) | async-done | bytes 262160 | tf_op jit(solution)/shard_map/reduce_scatter | solution.py:361
  1281.5 69.1 %reduce-scatter.25.cloned.1.call-done = bf16[256,512]{1,0:T(8,128)(2,1)} async-done(((bf16[2048,512]{1,0:T(8,128)(2,1)}), bf16[256,512]{1,0:T(8,128)(2,1)}) %reduce-scatter.25.cloned.1.call-update) | async-done | bytes 262160 | tf_op jit(solution)/shard_map/reduce_scatter | solution.py:364
  1352.4 44.2 %reduce-scatter.21.cloned.1.call-done = bf16[256,2048]{1,0:T(8,128)(2,1)} async-done(((bf16[1024,2048]{1,0:T(8,128)(2,1)}), bf16[256,2048]{1,0:T(8,128)(2,1)}) %reduce-scatter.21.cloned.1.call-update) | async-done | bytes 1048592 | tf_op jit(solution)/shard_map/reduce_scatter | solution.py:347
  1398.5 151.1 %reduce-scatter.17.cloned.1.call-done = bf16[256,2048]{1,0:T(8,128)(2,1)} async-done(((bf16[2048,2048]{1,0:T(8,128)(2,1)}), bf16[256,2048]{1,0:T(8,128)(2,1)}) %reduce-scatter.17.cloned.1.call-update) | async-done | bytes 1048592 | tf_op jit(solution)/shard_map/reduce_scatter | solution.py:247
  1555.9 39.5 %all-reduce = (f32[2048]{0:T(1024)}, f32[128]{0:T(128)}, f32[128]{0:T(128)}, f32[2048]{0:T(1024)}) all-reduce(f32[2048]{0:T(1024)S(1)} %get-tuple-element.249, f32[128]{0:T(128)S(1)} %bitcast_reduce_fusion.1, f32[128]{0:T(128)S(1)} %bitcast_reduce_fusion, ...), channel_id=1, replica_groups=mesh['expert'=8,'tensor'=4] {'expert','tensor'}, use_global_device_ids=true, to_apply=%region_29.30 | all-reduce | flops 4352 | bytes 34816 | tf_op jit(solution)/shard_map/psum | solution.py:374
  (341 shorter events, 497.1 us)
Async XLA Ops:
  8.0 42.1 %all-gather.4.cloned.1.call-start = ((), (), s32[]{:S(2)}) async-start(), calls=%async_computation.15 | async-start | bytes 5242880 | tf_op jit(solution)/shard_map/all_gather | solution.py:133
  12.8 139.1 %reduce-scatter.15.cloned.1.call-start = ((), (), s32[]{:S(2)}) async-start(), calls=%async_computation.16 | async-start | bytes 5242880 | tf_op jit(solution)/shard_map/reduce_scatter | solution.py:168
  107.2 315.0 %all-gather.6.cloned.1.call-start = ((), (), s32[]{:S(2)}) async-start(), calls=%async_computation.18 | async-start | bytes 9437184 | tf_op jit(solution)/shard_map/all_gather | solution.py:129
  185.0 44.3 %collective-permute-start.1 = (bf16[256,2048]{1,0:T(8,128)(2,1)S(1)}, bf16[256,2048]{1,0:T(8,128)(2,1)}, u32[]{:S(2)}, u32[]{:S(2)}) collective-permute-start(bf16[256,2048]{1,0:T(8,128)(2,1)S(1)} %collective-permute-done), channel_id=1, source_target_pairs={{0,4},{4,8},{8,12},{12,16},{16,20},{20,24},{24,28},{28,0},{1,5},{5... | collective-permute-start | bytes 3145736 | tf_op jit(solution)/shard_map/ppermute | solution.py:33
  185.0 46.9 %collective-permute-start.4 = (bf16[256,2048]{1,0:T(8,128)(2,1)}, bf16[256,2048]{1,0:T(8,128)(2,1)}, u32[]{:S(2)}, u32[]{:S(2)}) collective-permute-start(bf16[256,2048]{1,0:T(8,128)(2,1)} %fusion.83), channel_id=1, source_target_pairs={{4,0},{8,4},{12,8},{16,12},{20,16},{24,20},{28,24},{0,28},{5,1},{9... | collective-permute-start | bytes 3145736 | tf_op jit(solution)/shard_map/ppermute | solution.py:36
  229.3 57.5 %collective-permute-start.2 = (bf16[256,2048]{1,0:T(8,128)(2,1)}, bf16[256,2048]{1,0:T(8,128)(2,1)}, u32[]{:S(2)}, u32[]{:S(2)}) collective-permute-start(bf16[256,2048]{1,0:T(8,128)(2,1)} %collective-permute-done.1), channel_id=1, source_target_pairs={{0,4},{4,8},{8,12},{12,16},{16,20},{20,24},{24,28},{28,0},{1,5},{5... | collective-permute-start | bytes 3145736 | tf_op jit(solution)/shard_map/ppermute | solution.py:33
  231.9 57.4 %collective-permute-start.5 = (bf16[256,2048]{1,0:T(8,128)(2,1)}, bf16[256,2048]{1,0:T(8,128)(2,1)}, u32[]{:S(2)}, u32[]{:S(2)}) collective-permute-start(bf16[256,2048]{1,0:T(8,128)(2,1)} %collective-permute-done.4), channel_id=1, source_target_pairs={{4,0},{8,4},{12,8},{16,12},{20,16},{24,20},{28,24},{0,28},{5,1},{9... | collective-permute-start | bytes 3145736 | tf_op jit(solution)/shard_map/ppermute | solution.py:36
  286.8 55.8 %collective-permute-start.3 = (bf16[256,2048]{1,0:T(8,128)(2,1)}, bf16[256,2048]{1,0:T(8,128)(2,1)}, u32[]{:S(2)}, u32[]{:S(2)}) collective-permute-start(bf16[256,2048]{1,0:T(8,128)(2,1)} %collective-permute-done.2), channel_id=1, source_target_pairs={{0,4},{4,8},{8,12},{12,16},{16,20},{20,24},{24,28},{28,0},{1,5},{5... | collective-permute-start | bytes 3145736 | tf_op jit(solution)/shard_map/ppermute | solution.py:33
  289.3 68.2 %collective-permute-start.6 = (bf16[256,2048]{1,0:T(8,128)(2,1)}, bf16[256,2048]{1,0:T(8,128)(2,1)S(1)}, u32[]{:S(2)}, u32[]{:S(2)}) collective-permute-start(bf16[256,2048]{1,0:T(8,128)(2,1)} %collective-permute-done.5), channel_id=1, source_target_pairs={{4,0},{8,4},{12,8},{16,12},{20,16},{24,20},{28,24},{0,28},{5,1},{9... | collective-permute-start | bytes 3145736 | tf_op jit(solution)/shard_map/ppermute | solution.py:36
  465.7 275.8 %reduce-scatter.19.cloned.1.call-start = ((), (), s32[]{:S(2)}) async-start(), calls=%async_computation.19 | async-start | bytes 9437184 | tf_op jit(solution)/shard_map/reduce_scatter | solution.py:233
  597.2 243.4 %all-gather.8.cloned.1.call-start = ((), (), s32[]{:S(2)}) async-start(), calls=%async_computation.20 | async-start | bytes 5242880 | tf_op jit(solution)/shard_map/all_gather | solution.py:275
  749.9 244.0 %reduce-scatter.33.cloned.1.call-start = ((), (), s32[]{:S(2)}) async-start(), calls=%async_computation.28 | async-start | bytes 5242880 | tf_op jit(solution)/shard_map/reduce_scatter | solution.py:252
  763.8 230.2 %reduce-scatter.31.cloned.1.call-start = ((), (), s32[]{:S(2)}) async-start(), calls=%async_computation.27 | async-start | bytes 5242880 | tf_op jit(solution)/shard_map/reduce_scatter | solution.py:252
  778.0 225.5 %reduce-scatter.37.cloned.1.call-start = ((), (), s32[]{:S(2)}) async-start(), calls=%async_computation.30 | async-start | bytes 5242880 | tf_op jit(solution)/shard_map/reduce_scatter | solution.py:252
  791.9 211.6 %reduce-scatter.35.cloned.1.call-start = ((), (), s32[]{:S(2)}) async-start(), calls=%async_computation.29 | async-start | bytes 5242880 | tf_op jit(solution)/shard_map/reduce_scatter | solution.py:252
  807.0 213.2 %reduce-scatter.41.cloned.1.call-start = ((), (), s32[]{:S(2)}) async-start(), calls=%async_computation.32 | async-start | bytes 5242880 | tf_op jit(solution)/shard_map/reduce_scatter | solution.py:252
  823.9 243.6 %reduce-scatter.39.cloned.1.call-start = ((), (), s32[]{:S(2)}) async-start(), calls=%async_computation.31 | async-start | bytes 5242880 | tf_op jit(solution)/shard_map/reduce_scatter | solution.py:252
  840.5 298.7 %reduce-scatter.29.cloned.1.call-start = ((), (), s32[]{:S(2)}) async-start(), calls=%async_computation.25 | async-start | bytes 2359296 | tf_op jit(solution)/shard_map/reduce_scatter | solution.py:370
  854.4 355.1 %reduce-scatter.27.cloned.1.call-start = ((), (), s32[]{:S(2)}) async-start(), calls=%async_computation.24 | async-start | bytes 2359296 | tf_op jit(solution)/shard_map/reduce_scatter | solution.py:367
  894.9 384.8 %reduce-scatter.23.cloned.1.call-start = ((), (), s32[]{:S(2)}) async-start(), calls=%async_computation.22 | async-start | bytes 2359296 | tf_op jit(solution)/shard_map/reduce_scatter | solution.py:361
  918.4 432.3 %reduce-scatter.25.cloned.1.call-start = ((), (), s32[]{:S(2)}) async-start(), calls=%async_computation.23 | async-start | bytes 2359296 | tf_op jit(solution)/shard_map/reduce_scatter | solution.py:364
  934.7 461.9 %reduce-scatter.21.cloned.1.call-start = ((), (), s32[]{:S(2)}) async-start(), calls=%async_computation.21 | async-start | bytes 5242880 | tf_op jit(solution)/shard_map/reduce_scatter | solution.py:347
  946.5 603.1 %reduce-scatter.17.cloned.1.call-start = ((), (), s32[]{:S(2)}) async-start(), calls=%async_computation.17 | async-start | bytes 9437184 | tf_op jit(solution)/shard_map/reduce_scatter | solution.py:247
  989.3 606.1 %all-reduce.3.cloned.1.call-start = ((), (), s32[]{:S(2)}) async-start(), calls=%async_computation.26 | async-start | bytes 262144 | tf_op jit(solution)/shard_map/psum | solution.py:374
  (78 other events, 3483.3 us)
Sparse Core Ops, SparseCore 0:
  12.9 37.1 all-gather.3
  107.4 44.5 reduce-scatter.14
  750.0 33.5 all-gather.7
  786.1 44.5 reduce-scatter.32
  833.7 44.5 reduce-scatter.30
  881.2 44.5 reduce-scatter.36
  928.5 44.5 reduce-scatter.34
  975.6 44.5 reduce-scatter.40
  1022.9 44.5 reduce-scatter.38
  1070.9 68.2 reduce-scatter.28
  1142.8 66.7 reduce-scatter.26
  1212.9 66.7 reduce-scatter.22
  1283.8 66.7 reduce-scatter.24
  1353.0 43.5 reduce-scatter.20
  1400.5 148.9 reduce-scatter.16
Sparse Core Ops, SparseCore 1:
  231.9 174.2 all-gather.5
  597.3 144.2 reduce-scatter.18
  995.9 159.5 all-reduce.2
